TPU v7x, 32 devices: a whole 2x2x4 slice. The times are simulated.
32 devices in a mesh: slab: 16 (over z, y, x), sub: 2 (over core).
Axes of the slice: x: 2, y: 2, z: 4, core: 2. Of those that a mesh axis runs over, the one named last changes fastest.
Arguments:
- position: float32 [3, 8192, 128], P(None, ('slab', 'sub')), may hold values from -6 to 6
- state: int32 [8192, 128], P(('slab', 'sub')), may hold values from 0 to 2, as said below
- neighbours: int32 [8192, 8], P(('slab', 'sub')), may hold values from 0 to 8191, as said below
- voxel: int32 [8192, 128], P(('slab', 'sub')), may hold values from 0 to 4194303, as said below
- substrate: float32 [128, 128, 256], P('slab', 'sub'), may hold values from 0.5 to 1.5
- secretion: float32 [128, 128, 256], P('slab', 'sub'), may hold values from 0.2 to 4
Outputs:
- new_position: float32 [3, 8192, 128], P(None, ('slab', 'sub'))
- new_substrate: float32 [128, 128, 256], P('slab', 'sub')
- necrotic_fraction: float32 [], replicated
Inputs may be any that keep to these rules, and one draw needn't show every extreme that they name: `state`: 0 marks an empty slot, 1 a live cell, 2 a necrotic cell. `neighbours`: with tiles in blocks of 256 (block t // 256, its slab the block // 2, its part the block % 2): tile t lists itself first, then 8 - 1 different other tiles, each of its own block, of the last 32 tiles of the block 2 blocks before, or of the first 32 tiles of the block 2 blocks after. `voxel`: the cells of a tile of slab s and part u lie in voxels with x from s * 8 to s * 8 + 7 and y from u * 64 to u * 64 + 63.
All inputs are finite; a program needn't handle non-finite values.
Results may differ from a plain program's by a relative error of at most 0.00002.
Values sent between devices are 32-bit elements; how exact they have to be, the bound alone decides.
A program may use at most 64 MiB of HBM per device.

v0:
```python
import jax
import jax.numpy as jnp
from jax import lax
from jax.sharding import PartitionSpec as P

TILE = 128
NB = 8
GHOST = 32
SWEEPS = 8


SOFTENING = 0.01
REPEL_RADIUS = 2.0
ADHERE_RADIUS = 3.0
REPEL_STRENGTH = 0.05
ADHERE_STRENGTH = 0.02
SPEED_LIMIT = 0.2
SPEED_EPSILON = 1e-06
SUBSTRATE_STEP = 0.5
DECAY_RATE = 0.1
DIFFUSION_NUMBER = 2.0
UPTAKE_SCALE = 0.25


def with_halo(x, sides, width):
    for axis, dim in sides:
        size, length = (lax.axis_size(axis), x.shape[dim])
        up = [(i, (i + 1) % size) for i in range(size - 1)]
        down = [(j, i) for i, j in up]
        last = lax.slice_in_dim(x, length - width, length, axis=dim)
        initial = lax.slice_in_dim(x, 0, width, axis=dim)
        before = lax.ppermute(last, axis, up)
        after = lax.ppermute(initial, axis, down)
        x = jnp.concatenate([before, x, after], axis=dim)
    return x


def pair_forces(own_tiles, others):
    delta_x = own_tiles[0][:, :, None] - others[0][:, None, :]
    delta_y = own_tiles[1][:, :, None] - others[1][:, None, :]
    delta_z = own_tiles[2][:, :, None] - others[2][:, None, :]
    distance = jnp.sqrt(delta_x * delta_x + delta_y * delta_y + delta_z * delta_z + SOFTENING)
    repel = REPEL_STRENGTH * jnp.square(jnp.maximum(0.0, 1.0 - distance / REPEL_RADIUS))
    adhere = (
        ADHERE_STRENGTH
        * jnp.square(jnp.maximum(0.0, 1.0 - distance / ADHERE_RADIUS))
        * (own_tiles[4][:, :, None] * others[4][:, None, :])
    )
    weight = own_tiles[3][:, :, None] * others[3][:, None, :] * (repel - adhere) / distance
    return jnp.stack(
        [
            jnp.sum(weight * delta_x, -1),
            jnp.sum(weight * delta_y, -1),
            jnp.sum(weight * delta_z, -1),
        ],
        0,
    )


def neighbour_sum(padded):
    center = padded[1:-1, 1:-1]
    along_z = jnp.pad(center, ((0, 0), (0, 0), (1, 1)))
    return (
        padded[2:, 1:-1]
        + padded[:-2, 1:-1]
        + padded[1:-1, 2:]
        + padded[1:-1, :-2]
        + along_z[:, :, 2:]
        + along_z[:, :, :-2]
    )


def body(position, state, neighbours, voxel, substrate, secretion):
    tiles_dev = position.shape[1]
    sub_count = lax.axis_size("sub")
    slab_count = lax.axis_size("slab")
    slab_index = lax.axis_index("slab")
    sub_index = lax.axis_index("sub")
    occupied = (state > 0).astype(jnp.float32)
    living = (state == 1).astype(jnp.float32)
    live_local = jnp.sum((state == 1).astype(jnp.int32))
    necrotic_local = jnp.sum((state == 2).astype(jnp.int32))
    live_sum, necrotic_sum = lax.psum((live_local, necrotic_local), ("slab", "sub"))
    live_float = live_sum.astype(jnp.float32)
    necrotic_float = necrotic_sum.astype(jnp.float32)
    features = jnp.concatenate([position, occupied[None], living[None]], 0)
    ghosted = with_halo(features, (("slab", 1),), GHOST)
    first_tile = (slab_index * sub_count + sub_index) * tiles_dev
    below_block = neighbours < first_tile
    above_block = neighbours >= first_tile + tiles_dev
    local_ids = jnp.where(
        below_block,
        neighbours - (first_tile - sub_count * tiles_dev) - (tiles_dev - GHOST),
        jnp.where(
            above_block,
            GHOST + tiles_dev + neighbours - (first_tile + sub_count * tiles_dev),
            GHOST + neighbours - first_tile,
        ),
    )
    group_size = 4
    while tiles_dev % (2 * group_size) == 0 and tiles_dev // group_size > 16:
        group_size = 2 * group_size
    rounds = tiles_dev // group_size
    own_blocks = features.reshape(5, rounds, group_size, TILE).transpose(1, 0, 2, 3)
    id_blocks = local_ids.reshape(rounds, group_size, NB)

    def one_block(block_item):
        own_tiles, tile_ids = block_item
        others = jnp.take(ghosted, tile_ids.reshape(-1), axis=1).reshape(5, group_size, NB * TILE)
        return pair_forces(own_tiles, others)

    forces = lax.map(one_block, (own_blocks, id_blocks))
    velocity = forces.transpose(1, 0, 2, 3).reshape(3, tiles_dev, TILE)
    cell_speed = jnp.sqrt(jnp.sum(velocity * velocity, 0))
    local_fastest = jnp.max(cell_speed)
    fastest = lax.pmax(local_fastest, ("slab", "sub"))
    size_x, size_y, size_z = substrate.shape
    grid_y = size_y * sub_count
    grid_total = size_x * slab_count * grid_y * size_z
    per_cell = UPTAKE_SCALE * grid_total / live_float
    voxel_x = voxel // (grid_y * size_z)
    voxel_y = voxel // size_z % grid_y
    voxel_z = voxel % size_z
    local_flat = (
        (voxel_x - slab_index * size_x) * size_y + (voxel_y - sub_index * size_y)
    ) * size_z + voxel_z
    cell_count = (
        jnp.zeros((size_x * size_y * size_z,), jnp.float32)
        .at[local_flat.reshape(-1)]
        .add(living.reshape(-1))
        .reshape(size_x, size_y, size_z)
    )
    diagonal = 1.0 + SUBSTRATE_STEP * DECAY_RATE + 6.0 * DIFFUSION_NUMBER + per_cell * cell_count
    right_side = substrate + SUBSTRATE_STEP * secretion
    concentration = substrate
    margin_terms = with_halo(jnp.stack([right_side, diagonal]), (("slab", 1), ("sub", 2)), 2)
    row_index = slab_index * size_x - 1 + jnp.arange(size_x + 2)
    column_index = sub_index * size_y - 1 + jnp.arange(size_y + 2)
    inside_x = (row_index >= 0) & (row_index < size_x * slab_count)
    inside_y = (column_index >= 0) & (column_index < grid_y)
    inside = inside_x[:, None, None] & inside_y[None, :, None]
    right_margin = margin_terms[0][1:-1, 1:-1]
    diagonal_margin = jnp.where(inside, margin_terms[1][1:-1, 1:-1], 1.0)
    for pair_index in range(SWEEPS // 2):
        padded = with_halo(concentration, (("slab", 0), ("sub", 1)), 2)
        middle = jnp.where(
            inside, (right_margin + DIFFUSION_NUMBER * neighbour_sum(padded)) / diagonal_margin, 0.0
        )
        concentration = (right_side + DIFFUSION_NUMBER * neighbour_sum(middle)) / diagonal
    step_size = SPEED_LIMIT / (fastest + SPEED_EPSILON)
    new_position = position + step_size * velocity
    necrotic_fraction = necrotic_float / (live_float + necrotic_float)
    return (new_position, concentration, necrotic_fraction)


def solution(mesh):
    return jax.shard_map(
        body,
        mesh=mesh,
        in_specs=(
            P(None, ("slab", "sub"), None),
            P(("slab", "sub"), None),
            P(("slab", "sub"), None),
            P(("slab", "sub"), None),
            P("slab", "sub", None),
            P("slab", "sub", None),
        ),
        out_specs=(P(None, ("slab", "sub"), None), P("slab", "sub", None), P()),
        check_vma=False,
    )
```

profile of v0, /device:TPU:0, one launch (start us, length us, event | category | flops | bytes accessed | tf_op | source)
XLA Modules:
  0.0 674.5 jit_solution(15145228948525169444)
XLA Ops:
  1.7 4.9 collective-permute-start.6
  6.6 1.3 collective-permute-start.7
  7.9 1.6 convert_reduce_fusion.1
  10.4 1.3 copy.19
  12.6 5.2 collective-permute-start
  19.5 43.9 %all-reduce.8 = (s32[]{:T(128)}, s32[]{:T(128)}) all-reduce(s32[]{:T(128)} %get-tuple-element.61, s32[]{:T(128)} %get-tuple-element.94), channel_id=1, replica_groups=mesh['slab'=16,'sub'=2] {'slab','sub'}, use_global_device_ids=true, to_apply=%region_9.10 | all-reduce | flops 2 | bytes 16 | tf_op jit(solution)/shard_map/psum | solution.py:83
  64.1 171.2 %scatter_custom_fusion = f32[131072]{0:T(1024)S(1)} fusion(s32[32768]{0:T(1024)S(1)} %bitcast.76, f32[32768]{0:T(1024)S(1)} %get-tuple-element.95, f32[]{:T(128)} %constant.128.clone.1), kind=kCustom, calls=%fused_computation.158 | custom fusion | flops 32768 | bytes 524292 | tf_op jit(solution)/shard_map/scatter-add | solution.py:130
  236.6 4.2 collective-permute-start.2
  240.8 1.3 collective-permute-start.3
  242.2 1.3 collective-permute-start.8
  243.5 6.9 %collective-permute-done.2 = f32[2,2,64,256]{3,2,1,0:T(8,128)S(1)} collective-permute-done((f32[2,2,64,256]{3,2,1,0:T(8,128)S(1)}, f32[2,2,64,256]{3,2,1,0:T(8,128)S(1)}, u32[]{:S(2)}, u32[]{:S(2)}) %collective-permute-start.2) | collective-permute-done | bytes 262176 | tf_op jit(solution)/shard_map/ppermute | solution.py:32
  251.9 2.8 collective-permute-start.4
  254.7 1.3 collective-permute-start.5
  256.2 1.6 collective-permute-done.5
  260.1 5.0 collective-permute-start.10
  267.8 2.0 maximum_bitcast_fusion.1
  269.9 2.7 collective-permute-done.11
  274.7 1.3 collective-permute-start.13
  276.0 2.4 pad_maximum_fusion.1
  279.6 1.6 fusion.20
  283.2 2.5 collective-permute-start.14
  285.7 1.3 collective-permute-start.15
  287.0 314.4 %while.10 = (s32[]{:T(128)}, f32[16,3,16,128]{3,2,1,0:T(8,128)}, f32[16,5,16,128]{3,2,0,1:T(8,128)}, s32[16,16,8]{2,1,0:T(8,128)}, f32[5,320,128]{2,0,1:T(8,128)}, /*index=5*/s32[]{:T(128)}) while((s32[]{:T(128)}, f32[16,3,16,128]{3,2,1,0:T(8,128)}, f32[16,5,16,128]{3,2,0,1:T(8,128)}, s32[16,16,8]{2,1,0:T(8,128)}, f32[5,320,128]{2,0,1:T(8,128)}, ...), condition=%wide.region_4.5_spmd, body=%wide.region_0.4_spmd.sunk | while | flops 65101952 | bytes 3238221 | solution.py:112
  287.8 2.0 gather_fusion
  291.9 14.1 %fusion.82 = (f32[16,128]{1,0:T(8,128)S(1)}, f32[16,128]{1,0:T(8,128)S(1)}, f32[16,128]{1,0:T(8,128)S(1)}) fusion(f32[16,1024]{1,0:T(8,128)S(1)} %sub.306, f32[16,128]{1,0:T(8,128)S(1)} %get-tuple-element.142, f32[16,1024]{1,0:T(8,128)S(1)} %mul.388, f32[16,128]{1,0:T(8,128)S(1)} %get-tuple-element.144, f32[16,1024]{1,0:T(8,128)S(1)} %sub.307, ...), kind=kLoop, calls=%fused_computation.12.clone.1 | loop fusion | flops 65005568 | bytes 393216 | tf_op jit(solution)/shard_map/while/body/eval_jaxpr/reduce_sum | solution.py:52
  307.4 2.0 gather_fusion
  311.5 14.1 %fusion.82 = (f32[16,128]{1,0:T(8,128)S(1)}, f32[16,128]{1,0:T(8,128)S(1)}, f32[16,128]{1,0:T(8,128)S(1)}) fusion(f32[16,1024]{1,0:T(8,128)S(1)} %sub.306, f32[16,128]{1,0:T(8,128)S(1)} %get-tuple-element.142, f32[16,1024]{1,0:T(8,128)S(1)} %mul.388, f32[16,128]{1,0:T(8,128)S(1)} %get-tuple-element.144, f32[16,1024]{1,0:T(8,128)S(1)} %sub.307, ...), kind=kLoop, calls=%fused_computation.12.clone.1 | loop fusion | flops 65005568 | bytes 393216 | tf_op jit(solution)/shard_map/while/body/eval_jaxpr/reduce_sum | solution.py:52
  327.1 2.0 gather_fusion
  331.2 14.1 %fusion.82 = (f32[16,128]{1,0:T(8,128)S(1)}, f32[16,128]{1,0:T(8,128)S(1)}, f32[16,128]{1,0:T(8,128)S(1)}) fusion(f32[16,1024]{1,0:T(8,128)S(1)} %sub.306, f32[16,128]{1,0:T(8,128)S(1)} %get-tuple-element.142, f32[16,1024]{1,0:T(8,128)S(1)} %mul.388, f32[16,128]{1,0:T(8,128)S(1)} %get-tuple-element.144, f32[16,1024]{1,0:T(8,128)S(1)} %sub.307, ...), kind=kLoop, calls=%fused_computation.12.clone.1 | loop fusion | flops 65005568 | bytes 393216 | tf_op jit(solution)/shard_map/while/body/eval_jaxpr/reduce_sum | solution.py:52
  346.7 2.0 gather_fusion
  350.8 14.1 %fusion.82 = (f32[16,128]{1,0:T(8,128)S(1)}, f32[16,128]{1,0:T(8,128)S(1)}, f32[16,128]{1,0:T(8,128)S(1)}) fusion(f32[16,1024]{1,0:T(8,128)S(1)} %sub.306, f32[16,128]{1,0:T(8,128)S(1)} %get-tuple-element.142, f32[16,1024]{1,0:T(8,128)S(1)} %mul.388, f32[16,128]{1,0:T(8,128)S(1)} %get-tuple-element.144, f32[16,1024]{1,0:T(8,128)S(1)} %sub.307, ...), kind=kLoop, calls=%fused_computation.12.clone.1 | loop fusion | flops 65005568 | bytes 393216 | tf_op jit(solution)/shard_map/while/body/eval_jaxpr/reduce_sum | solution.py:52
  366.4 2.0 gather_fusion
  370.5 14.1 %fusion.82 = (f32[16,128]{1,0:T(8,128)S(1)}, f32[16,128]{1,0:T(8,128)S(1)}, f32[16,128]{1,0:T(8,128)S(1)}) fusion(f32[16,1024]{1,0:T(8,128)S(1)} %sub.306, f32[16,128]{1,0:T(8,128)S(1)} %get-tuple-element.142, f32[16,1024]{1,0:T(8,128)S(1)} %mul.388, f32[16,128]{1,0:T(8,128)S(1)} %get-tuple-element.144, f32[16,1024]{1,0:T(8,128)S(1)} %sub.307, ...), kind=kLoop, calls=%fused_computation.12.clone.1 | loop fusion | flops 65005568 | bytes 393216 | tf_op jit(solution)/shard_map/while/body/eval_jaxpr/reduce_sum | solution.py:52
  386.0 2.0 gather_fusion
  390.1 14.1 %fusion.82 = (f32[16,128]{1,0:T(8,128)S(1)}, f32[16,128]{1,0:T(8,128)S(1)}, f32[16,128]{1,0:T(8,128)S(1)}) fusion(f32[16,1024]{1,0:T(8,128)S(1)} %sub.306, f32[16,128]{1,0:T(8,128)S(1)} %get-tuple-element.142, f32[16,1024]{1,0:T(8,128)S(1)} %mul.388, f32[16,128]{1,0:T(8,128)S(1)} %get-tuple-element.144, f32[16,1024]{1,0:T(8,128)S(1)} %sub.307, ...), kind=kLoop, calls=%fused_computation.12.clone.1 | loop fusion | flops 65005568 | bytes 393216 | tf_op jit(solution)/shard_map/while/body/eval_jaxpr/reduce_sum | solution.py:52
  405.7 2.0 gather_fusion
  409.8 14.1 %fusion.82 = (f32[16,128]{1,0:T(8,128)S(1)}, f32[16,128]{1,0:T(8,128)S(1)}, f32[16,128]{1,0:T(8,128)S(1)}) fusion(f32[16,1024]{1,0:T(8,128)S(1)} %sub.306, f32[16,128]{1,0:T(8,128)S(1)} %get-tuple-element.142, f32[16,1024]{1,0:T(8,128)S(1)} %mul.388, f32[16,128]{1,0:T(8,128)S(1)} %get-tuple-element.144, f32[16,1024]{1,0:T(8,128)S(1)} %sub.307, ...), kind=kLoop, calls=%fused_computation.12.clone.1 | loop fusion | flops 65005568 | bytes 393216 | tf_op jit(solution)/shard_map/while/body/eval_jaxpr/reduce_sum | solution.py:52
  425.3 2.0 gather_fusion
  429.4 14.1 %fusion.82 = (f32[16,128]{1,0:T(8,128)S(1)}, f32[16,128]{1,0:T(8,128)S(1)}, f32[16,128]{1,0:T(8,128)S(1)}) fusion(f32[16,1024]{1,0:T(8,128)S(1)} %sub.306, f32[16,128]{1,0:T(8,128)S(1)} %get-tuple-element.142, f32[16,1024]{1,0:T(8,128)S(1)} %mul.388, f32[16,128]{1,0:T(8,128)S(1)} %get-tuple-element.144, f32[16,1024]{1,0:T(8,128)S(1)} %sub.307, ...), kind=kLoop, calls=%fused_computation.12.clone.1 | loop fusion | flops 65005568 | bytes 393216 | tf_op jit(solution)/shard_map/while/body/eval_jaxpr/reduce_sum | solution.py:52
  445.0 2.0 gather_fusion
  449.0 14.1 %fusion.82 = (f32[16,128]{1,0:T(8,128)S(1)}, f32[16,128]{1,0:T(8,128)S(1)}, f32[16,128]{1,0:T(8,128)S(1)}) fusion(f32[16,1024]{1,0:T(8,128)S(1)} %sub.306, f32[16,128]{1,0:T(8,128)S(1)} %get-tuple-element.142, f32[16,1024]{1,0:T(8,128)S(1)} %mul.388, f32[16,128]{1,0:T(8,128)S(1)} %get-tuple-element.144, f32[16,1024]{1,0:T(8,128)S(1)} %sub.307, ...), kind=kLoop, calls=%fused_computation.12.clone.1 | loop fusion | flops 65005568 | bytes 393216 | tf_op jit(solution)/shard_map/while/body/eval_jaxpr/reduce_sum | solution.py:52
  464.6 2.0 gather_fusion
  468.7 14.1 %fusion.82 = (f32[16,128]{1,0:T(8,128)S(1)}, f32[16,128]{1,0:T(8,128)S(1)}, f32[16,128]{1,0:T(8,128)S(1)}) fusion(f32[16,1024]{1,0:T(8,128)S(1)} %sub.306, f32[16,128]{1,0:T(8,128)S(1)} %get-tuple-element.142, f32[16,1024]{1,0:T(8,128)S(1)} %mul.388, f32[16,128]{1,0:T(8,128)S(1)} %get-tuple-element.144, f32[16,1024]{1,0:T(8,128)S(1)} %sub.307, ...), kind=kLoop, calls=%fused_computation.12.clone.1 | loop fusion | flops 65005568 | bytes 393216 | tf_op jit(solution)/shard_map/while/body/eval_jaxpr/reduce_sum | solution.py:52
  484.3 2.0 gather_fusion
  488.3 14.1 %fusion.82 = (f32[16,128]{1,0:T(8,128)S(1)}, f32[16,128]{1,0:T(8,128)S(1)}, f32[16,128]{1,0:T(8,128)S(1)}) fusion(f32[16,1024]{1,0:T(8,128)S(1)} %sub.306, f32[16,128]{1,0:T(8,128)S(1)} %get-tuple-element.142, f32[16,1024]{1,0:T(8,128)S(1)} %mul.388, f32[16,128]{1,0:T(8,128)S(1)} %get-tuple-element.144, f32[16,1024]{1,0:T(8,128)S(1)} %sub.307, ...), kind=kLoop, calls=%fused_computation.12.clone.1 | loop fusion | flops 65005568 | bytes 393216 | tf_op jit(solution)/shard_map/while/body/eval_jaxpr/reduce_sum | solution.py:52
  503.9 2.0 gather_fusion
  508.0 14.1 %fusion.82 = (f32[16,128]{1,0:T(8,128)S(1)}, f32[16,128]{1,0:T(8,128)S(1)}, f32[16,128]{1,0:T(8,128)S(1)}) fusion(f32[16,1024]{1,0:T(8,128)S(1)} %sub.306, f32[16,128]{1,0:T(8,128)S(1)} %get-tuple-element.142, f32[16,1024]{1,0:T(8,128)S(1)} %mul.388, f32[16,128]{1,0:T(8,128)S(1)} %get-tuple-element.144, f32[16,1024]{1,0:T(8,128)S(1)} %sub.307, ...), kind=kLoop, calls=%fused_computation.12.clone.1 | loop fusion | flops 65005568 | bytes 393216 | tf_op jit(solution)/shard_map/while/body/eval_jaxpr/reduce_sum | solution.py:52
  523.6 2.0 gather_fusion
  527.6 14.1 %fusion.82 = (f32[16,128]{1,0:T(8,128)S(1)}, f32[16,128]{1,0:T(8,128)S(1)}, f32[16,128]{1,0:T(8,128)S(1)}) fusion(f32[16,1024]{1,0:T(8,128)S(1)} %sub.306, f32[16,128]{1,0:T(8,128)S(1)} %get-tuple-element.142, f32[16,1024]{1,0:T(8,128)S(1)} %mul.388, f32[16,128]{1,0:T(8,128)S(1)} %get-tuple-element.144, f32[16,1024]{1,0:T(8,128)S(1)} %sub.307, ...), kind=kLoop, calls=%fused_computation.12.clone.1 | loop fusion | flops 65005568 | bytes 393216 | tf_op jit(solution)/shard_map/while/body/eval_jaxpr/reduce_sum | solution.py:52
  543.2 2.0 gather_fusion
  547.3 14.1 %fusion.82 = (f32[16,128]{1,0:T(8,128)S(1)}, f32[16,128]{1,0:T(8,128)S(1)}, f32[16,128]{1,0:T(8,128)S(1)}) fusion(f32[16,1024]{1,0:T(8,128)S(1)} %sub.306, f32[16,128]{1,0:T(8,128)S(1)} %get-tuple-element.142, f32[16,1024]{1,0:T(8,128)S(1)} %mul.388, f32[16,128]{1,0:T(8,128)S(1)} %get-tuple-element.144, f32[16,1024]{1,0:T(8,128)S(1)} %sub.307, ...), kind=kLoop, calls=%fused_computation.12.clone.1 | loop fusion | flops 65005568 | bytes 393216 | tf_op jit(solution)/shard_map/while/body/eval_jaxpr/reduce_sum | solution.py:52
  562.9 2.0 gather_fusion
  566.9 14.1 %fusion.82 = (f32[16,128]{1,0:T(8,128)S(1)}, f32[16,128]{1,0:T(8,128)S(1)}, f32[16,128]{1,0:T(8,128)S(1)}) fusion(f32[16,1024]{1,0:T(8,128)S(1)} %sub.306, f32[16,128]{1,0:T(8,128)S(1)} %get-tuple-element.142, f32[16,1024]{1,0:T(8,128)S(1)} %mul.388, f32[16,128]{1,0:T(8,128)S(1)} %get-tuple-element.144, f32[16,1024]{1,0:T(8,128)S(1)} %sub.307, ...), kind=kLoop, calls=%fused_computation.12.clone.1 | loop fusion | flops 65005568 | bytes 393216 | tf_op jit(solution)/shard_map/while/body/eval_jaxpr/reduce_sum | solution.py:52
  582.5 2.0 gather_fusion
  586.6 14.1 %fusion.82 = (f32[16,128]{1,0:T(8,128)S(1)}, f32[16,128]{1,0:T(8,128)S(1)}, f32[16,128]{1,0:T(8,128)S(1)}) fusion(f32[16,1024]{1,0:T(8,128)S(1)} %sub.306, f32[16,128]{1,0:T(8,128)S(1)} %get-tuple-element.142, f32[16,1024]{1,0:T(8,128)S(1)} %mul.388, f32[16,128]{1,0:T(8,128)S(1)} %get-tuple-element.144, f32[16,1024]{1,0:T(8,128)S(1)} %sub.307, ...), kind=kLoop, calls=%fused_computation.12.clone.1 | loop fusion | flops 65005568 | bytes 393216 | tf_op jit(solution)/shard_map/while/body/eval_jaxpr/reduce_sum | solution.py:52
  602.5 1.5 pad_maximum_fusion.40
  604.0 2.7 collective-permute-start.16
  606.8 1.5 collective-permute-start.17
  609.0 42.4 %pmax.7 = f32[]{:T(128)} all-reduce(f32[]{:T(128)} %sqrt_reduce_fusion), channel_id=1, replica_groups=mesh['slab'=16,'sub'=2] {'slab','sub'}, use_global_device_ids=true, to_apply=%region_7.8 | all-reduce | flops 1 | bytes 8 | tf_op jit(solution)/shard_map/pmax | solution.py:116
  653.1 1.6 fusion.26
  655.2 4.3 collective-permute-start.18
  659.5 1.3 collective-permute-start.19
  662.0 4.8 collective-permute-done.19
  668.2 1.3 collective-permute-start.21
  (352 shorter events, 81.9 us)
Async XLA Ops:
  0.6 18.4 %copy-start.9 = (s32[256,128]{1,0:T(8,128)S(1)}, s32[256,128]{1,0:T(8,128)}, u32[]{:S(2)}) copy-start(s32[256,128]{1,0:T(8,128)} %param.11) | copy-start | bytes 393220
  1.7 234.1 %collective-permute-start.6 = (f32[2,64,256]{2,1,0:T(8,128)S(1)}, f32[2,64,256]{2,1,0:T(8,128)S(1)}, u32[]{:S(2)}, u32[]{:S(2)}) collective-permute-start(f32[2,64,256]{2,1,0:T(8,128)S(1)} %get-tuple-element.91), channel_id=1, source_target_pairs={{0,2},{2,4},{4,6},{6,8},{8,10},{10,12},{12,14},{14,16},{16,18},{18... | collective-permute-start | bytes 393224 | tf_op jit(solution)/shard_map/ppermute | solution.py:32
  6.6 235.6 %collective-permute-start.7 = (f32[2,64,256]{2,1,0:T(8,128)S(1)}, f32[2,64,256]{2,1,0:T(8,128)S(1)}, u32[]{:S(2)}, u32[]{:S(2)}) collective-permute-start(f32[2,64,256]{2,1,0:T(8,128)S(1)} %get-tuple-element.90), channel_id=1, source_target_pairs={{2,0},{4,2},{6,4},{8,6},{10,8},{12,10},{14,12},{16,14},{18,16},{20... | collective-permute-start | bytes 393224 | tf_op jit(solution)/shard_map/ppermute | solution.py:33
  10.4 53.7 %copy-start.5 = (f32[256,128]{1,0:T(8,128)}, f32[256,128]{1,0:T(8,128)S(1)}, u32[]{:S(2)}) copy-start(f32[256,128]{1,0:T(8,128)S(1)} %get-tuple-element.96) | copy-start | bytes 393220
  11.7 223.7 %copy-start.2 = (f32[3,256,128]{2,0,1:T(4,128)}, f32[3,256,128]{2,0,1:T(4,128)S(1)}, u32[]{:S(2)}) copy-start(f32[3,256,128]{2,0,1:T(4,128)S(1)} %copy.19) | copy-start | bytes 1179652
  12.6 263.4 %collective-permute-start = (f32[5,32,128]{2,0,1:T(8,128)}, f32[5,32,128]{2,0,1:T(8,128)}, u32[]{:S(2)}, u32[]{:S(2)}) collective-permute-start(f32[5,32,128]{2,0,1:T(8,128)} %get-tuple-element.82), channel_id=1, source_target_pairs={{0,2},{2,4},{4,6},{6,8},{8,10},{10,12},{12,14},{14,16},{16,18},{18... | collective-permute-start | bytes 245768 | tf_op jit(solution)/shard_map/ppermute | solution.py:32
  17.8 258.3 %collective-permute-start.1 = (f32[5,32,128]{2,0,1:T(8,128)}, f32[5,32,128]{2,0,1:T(8,128)}, u32[]{:S(2)}, u32[]{:S(2)}) collective-permute-start(f32[5,32,128]{2,0,1:T(8,128)} %get-tuple-element.83), channel_id=1, source_target_pairs={{2,0},{4,2},{6,4},{8,6},{10,8},{12,10},{14,12},{16,14},{18,16},{20... | collective-permute-start | bytes 245768 | tf_op jit(solution)/shard_map/ppermute | solution.py:33
  235.3 1.0 copy-start.7
  235.3 1.2 copy-start.8
  236.6 13.7 %collective-permute-start.2 = (f32[2,2,64,256]{3,2,1,0:T(8,128)S(1)}, f32[2,2,64,256]{3,2,1,0:T(8,128)S(1)}, u32[]{:S(2)}, u32[]{:S(2)}) collective-permute-start(f32[2,2,64,256]{3,2,1,0:T(8,128)S(1)} %get-tuple-element.72), channel_id=1, source_target_pairs={{0,2},{2,4},{4,6},{6,8},{8,10},{10,12},{12,14},{14,16},{16,18},{18... | collective-permute-start | bytes 786440 | tf_op jit(solution)/shard_map/ppermute | solution.py:32
  240.8 11.1 %collective-permute-start.3 = (f32[2,2,64,256]{3,2,1,0:T(8,128)S(1)}, f32[2,2,64,256]{3,2,1,0:T(8,128)S(1)}, u32[]{:S(2)}, u32[]{:S(2)}) collective-permute-start(f32[2,2,64,256]{3,2,1,0:T(8,128)S(1)} %get-tuple-element.73), channel_id=1, source_target_pairs={{2,0},{4,2},{6,4},{8,6},{10,8},{12,10},{14,12},{16,14},{18,16},{20... | collective-permute-start | bytes 786440 | tf_op jit(solution)/shard_map/ppermute | solution.py:33
  242.2 12.5 %collective-permute-start.8 = (f32[12,2,256]{2,1,0:T(2,128)S(1)}, f32[12,2,256]{2,1,0:T(2,128)S(1)}, u32[]{:S(2)}, u32[]{:S(2)}) collective-permute-start(f32[12,2,256]{2,1,0:T(2,128)S(1)} %get-tuple-element.80), channel_id=1, source_target_pairs={{0,1},{2,3},{4,5},{6,7},{8,9},{10,11},{12,13},{14,15},{16,17},{18,... | collective-permute-start | bytes 73736 | tf_op jit(solution)/shard_map/ppermute | solution.py:32
  250.3 5.7 collective-permute-start.9
  251.9 4.3 collective-permute-start.4
  254.7 3.1 collective-permute-start.5
  259.0 7.4 %copy-start.10 = (s32[256,8]{0,1:T(8,128)S(1)}, s32[256,8]{0,1:T(8,128)}, u32[]{:S(2)}) copy-start(s32[256,8]{0,1:T(8,128)} %param.10) | copy-start | bytes 24580
  260.1 9.8 %collective-permute-start.10 = (f32[2,64,256]{2,1,0:T(8,128)}, f32[2,64,256]{2,1,0:T(8,128)}, u32[]{:S(2)}, u32[]{:S(2)}) collective-permute-start(f32[2,64,256]{2,1,0:T(8,128)} %get-tuple-element.88), channel_id=1, source_target_pairs={{0,2},{2,4},{4,6},{6,8},{8,10},{10,12},{12,14},{14,16},{16,18},{18... | collective-permute-start | bytes 393224 | tf_op jit(solution)/shard_map/ppermute | solution.py:32
  265.1 7.5 %collective-permute-start.11 = (f32[2,64,256]{2,1,0:T(8,128)}, f32[2,64,256]{2,1,0:T(8,128)}, u32[]{:S(2)}, u32[]{:S(2)}) collective-permute-start(f32[2,64,256]{2,1,0:T(8,128)} %get-tuple-element.89), channel_id=1, source_target_pairs={{2,0},{4,2},{6,4},{8,6},{10,8},{12,10},{14,12},{16,14},{18,16},{20... | collective-permute-start | bytes 393224 | tf_op jit(solution)/shard_map/ppermute | solution.py:33
  267.8 8.2 %copy-start.3 = (f32[3,256,128]{2,0,1:T(4,128)S(1)}, f32[3,256,128]{2,0,1:T(4,128)}, u32[]{:S(2)}) copy-start(f32[3,256,128]{2,0,1:T(4,128)} %copy-done.2) | copy-start | bytes 1179652
  267.8 8.2 %copy-start.6 = (f32[256,128]{1,0:T(8,128)S(1)}, f32[256,128]{1,0:T(8,128)}, u32[]{:S(2)}) copy-start(f32[256,128]{1,0:T(8,128)} %copy-done.5) | copy-start | bytes 393220
  273.4 5.0 collective-permute-start.12
  274.7 3.7 collective-permute-start.13
  281.7 0.8 copy-start
  283.2 319.3 %collective-permute-start.14 = (f32[2,64,256]{2,1,0:T(8,128)}, f32[2,64,256]{2,1,0:T(8,128)S(1)}, u32[]{:S(2)}, u32[]{:S(2)}) collective-permute-start(f32[2,64,256]{2,1,0:T(8,128)} %get-tuple-element.86), channel_id=1, source_target_pairs={{0,2},{2,4},{4,6},{6,8},{8,10},{10,12},{12,14},{14,16},{16,18},{18... | collective-permute-start | bytes 393224 | tf_op jit(solution)/shard_map/ppermute | solution.py:32
  285.7 316.8 %collective-permute-start.15 = (f32[2,64,256]{2,1,0:T(8,128)}, f32[2,64,256]{2,1,0:T(8,128)}, u32[]{:S(2)}, u32[]{:S(2)}) collective-permute-start(f32[2,64,256]{2,1,0:T(8,128)} %get-tuple-element.87), channel_id=1, source_target_pairs={{2,0},{4,2},{6,4},{8,6},{10,8},{12,10},{14,12},{16,14},{18,16},{20... | collective-permute-start | bytes 393224 | tf_op jit(solution)/shard_map/ppermute | solution.py:33
  601.3 50.7 %copy-start.1 = (f32[8,64,256]{2,1,0:T(8,128)S(1)}, f32[8,64,256]{2,1,0:T(8,128)}, u32[]{:S(2)}) copy-start(f32[8,64,256]{2,1,0:T(8,128)} %copy-done) | copy-start | bytes 1572868
  604.0 48.0 %collective-permute-start.16 = (f32[12,2,256]{2,1,0:T(2,128)}, f32[12,2,256]{2,1,0:T(2,128)S(1)}, u32[]{:S(2)}, u32[]{:S(2)}) collective-permute-start(f32[12,2,256]{2,1,0:T(2,128)} %get-tuple-element.76), channel_id=1, source_target_pairs={{0,1},{2,3},{4,5},{6,7},{8,9},{10,11},{12,13},{14,15},{16,17},{18,... | collective-permute-start | bytes 73736 | tf_op jit(solution)/shard_map/ppermute | solution.py:32
  606.8 45.3 %collective-permute-start.17 = (f32[12,2,256]{2,1,0:T(2,128)}, f32[12,2,256]{2,1,0:T(2,128)S(1)}, u32[]{:S(2)}, u32[]{:S(2)}) collective-permute-start(f32[12,2,256]{2,1,0:T(2,128)} %get-tuple-element.77), channel_id=1, source_target_pairs={{1,0},{3,2},{5,4},{7,6},{9,8},{11,10},{13,12},{15,14},{17,16},{19,... | collective-permute-start | bytes 73736 | tf_op jit(solution)/shard_map/ppermute | solution.py:33
  655.2 14.3 %copy-start.4 = (f32[3,256,128]{2,1,0:T(8,128)S(1)}, f32[3,256,128]{2,1,0:T(8,128)}, u32[]{:S(2)}) copy-start(f32[3,256,128]{2,1,0:T(8,128)} %param.8) | copy-start | bytes 1179652
  655.2 6.8 %collective-permute-start.18 = (f32[2,64,256]{2,1,0:T(8,128)S(1)}, f32[2,64,256]{2,1,0:T(8,128)S(1)}, u32[]{:S(2)}, u32[]{:S(2)}) collective-permute-start(f32[2,64,256]{2,1,0:T(8,128)S(1)} %get-tuple-element.84), channel_id=1, source_target_pairs={{0,2},{2,4},{4,6},{6,8},{8,10},{10,12},{12,14},{14,16},{16,18},{18... | collective-permute-start | bytes 393224 | tf_op jit(solution)/shard_map/ppermute | solution.py:32
  659.5 7.3 %collective-permute-start.19 = (f32[2,64,256]{2,1,0:T(8,128)S(1)}, f32[2,64,256]{2,1,0:T(8,128)S(1)}, u32[]{:S(2)}, u32[]{:S(2)}) collective-permute-start(f32[2,64,256]{2,1,0:T(8,128)S(1)} %get-tuple-element.85), channel_id=1, source_target_pairs={{2,0},{4,2},{6,4},{8,6},{10,8},{12,10},{14,12},{16,14},{18,16},{20... | collective-permute-start | bytes 393224 | tf_op jit(solution)/shard_map/ppermute | solution.py:33
  666.9 3.4 collective-permute-start.20
  668.2 3.1 collective-permute-start.21
where the time goes:
time: 678 us; the launch traced here: 674 us
  other arithmetic  435 us (64%)
  blocking collectives  86.3 us (13%)
  local copies, waits for them, and re-layouts  80.3 us (12%)
  starting transfers between devices  49.8 us (7%)
  waiting for transfers between devices  17.5 us (3%)
    reduce_sum x16, other arithmetic, pair_forces(): jnp.sum(weight * delta_x, -1)  226 us
    scatter-add x1, other arithmetic, body(): cell_count = jnp.zeros((size_x * size_y * size_z,), jnp.float32).at[local...  171 us
    psum x1, blocking collectives, body(): lax.psum((live_local, necrotic_local), ('slab', 'sub'))  43.9 us
    pmax x1, blocking collectives, body(): fastest = lax.pmax(local_fastest, ('slab', 'sub'))  42.4 us
    ppermute x11, starting transfers between devices, with_halo(): before = lax.ppermute(last, axis, up)  35.4 us
    gather x16, local copies, waits for them, and re-layouts, one_block(): jnp.take(ghosted, tile_ids.reshape(-1), axis=1)  31.4 us
    dynamic_slice x32, local copies, waits for them, and re-layouts, body(): forces = lax.map(one_block, (own_blocks, id_blocks))  23.8 us
    ppermute x11, starting transfers between devices, with_halo(): after = lax.ppermute(initial, axis, down)  14.4 us
  transfers between devices with their start and end apart: 22, of which 7 were waited for; matrix products, arithmetic and copies ran while one was open for 74% of the time, Pallas kernels for 0%

commit v1 on v0

v1 whole, which is shorter than its diff:
```python
import jax
import jax.numpy as jnp
from jax import lax
from jax.experimental import pallas as pl
from jax.experimental.pallas import tpu as pltpu
from jax.sharding import PartitionSpec as P

TILE = 128
NB = 8
GHOST = 32
SWEEPS = 8


SOFTENING = 0.01
REPEL_RADIUS = 2.0
ADHERE_RADIUS = 3.0
REPEL_STRENGTH = 0.05
ADHERE_STRENGTH = 0.02
SPEED_LIMIT = 0.2
SPEED_EPSILON = 1e-06
SUBSTRATE_STEP = 0.5
DECAY_RATE = 0.1
DIFFUSION_NUMBER = 2.0
UPTAKE_SCALE = 0.25


def with_halo(x, sides, width):
    for axis, dim in sides:
        size, length = (lax.axis_size(axis), x.shape[dim])
        up = [(i, (i + 1) % size) for i in range(size - 1)]
        down = [(j, i) for i, j in up]
        last = lax.slice_in_dim(x, length - width, length, axis=dim)
        initial = lax.slice_in_dim(x, 0, width, axis=dim)
        before = lax.ppermute(last, axis, up)
        after = lax.ppermute(initial, axis, down)
        x = jnp.concatenate([before, x, after], axis=dim)
    return x


FAR = 1.0e6
ROWS = 8
K_ROWS = 64
Q_ROWS = 32
OCCUPIED_ROW = 3
LIMIT_ROW = 4


def split3(x):
    high = x.astype(jnp.bfloat16).astype(jnp.float32)
    rest = x - high
    middle = rest.astype(jnp.bfloat16).astype(jnp.float32)
    return high, middle, rest - middle


def force_rows(base, own):
    row = lax.broadcasted_iota(jnp.int32, base.shape, 0)
    half = jnp.where(row < 3, 0.5 * base, 0.0)
    square = jnp.sum(half * half, axis=0, keepdims=True)
    high, middle, low = split3(half)
    zero = jnp.zeros_like(base)
    if own:
        first, shift = 0, -2.0
    else:
        occupied = base[OCCUPIED_ROW:OCCUPIED_ROW + 1] > 0
        square = jnp.where(occupied, square + 0.25 * SOFTENING, FAR)
        first, shift = 3, 1.0
    norm = jnp.where(row < 6, 1.0, 0.0)
    for r, part in enumerate(split3(square)):
        norm = jnp.where(row == first + r, part, norm)
    if own:
        groups = [high, high, middle, high, low, middle]
    else:
        groups = [high, middle, high, low, high, middle]
    matrix = jnp.concatenate([shift * g for g in groups] + [norm, zero], 0)
    summed = jnp.concatenate([jnp.where(row == 3, 1.0, high), middle, low, zero], 0)
    return matrix.astype(jnp.bfloat16), summed.astype(jnp.bfloat16)


def force_kernel(group, ids, base_ref, out_ref, other_rows, summed_rows, weights, gathered,
                 own_limit):
    width = NB * TILE
    step = pl.program_id(0)

    @pl.when(step == 0)
    def _():
        @pl.loop(0, base_ref.shape[0])
        def _(tile):
            other_rows[tile], summed_rows[tile] = force_rows(base_ref[tile], False)

    for g in range(group):
        me = step * group + g
        own_base = base_ref[GHOST + me]
        own, _ = force_rows(own_base, True)
        own_limit[g] = jnp.broadcast_to(
            own_base[LIMIT_ROW:LIMIT_ROW + 1, :], (TILE, TILE)
        ).T
        for j in range(NB):
            tile = ids[me * NB + j]
            cols = slice(j * TILE, (j + 1) * TILE)
            lows = slice(width + j * TILE, width + (j + 1) * TILE)
            squared = lax.dot_general(
                own, other_rows[tile], (((0,), (0,)), ((), ())),
                preferred_element_type=jnp.float32,
            )
            inverse = lax.rsqrt(squared)
            half_distance = squared * inverse
            repel = jnp.maximum(0.0, 1.0 - half_distance)
            limit = jnp.minimum(own_limit[g], base_ref[tile, LIMIT_ROW:LIMIT_ROW + 1, :])
            adhere = jnp.maximum(0.0, limit - half_distance)
            ratio = ADHERE_STRENGTH / REPEL_STRENGTH * (REPEL_RADIUS / ADHERE_RADIUS) ** 2
            weight = (repel * repel - ratio * (adhere * adhere)) * inverse
            high = weight.astype(jnp.bfloat16)
            low = (weight - high.astype(jnp.float32)).astype(jnp.bfloat16)
            weights[g, :, cols] = high
            weights[g, :, lows] = low
            summed = summed_rows[tile]
            gathered[g, :, cols] = summed
            gathered[g, :, lows] = summed
        sums = lax.dot_general(
            weights[g], gathered[g], (((1,), (1,)), ((), ())),
            preferred_element_type=jnp.float32,
        ).T
        moment = sums[0:ROWS] + sums[ROWS:2 * ROWS] + sums[2 * ROWS:3 * ROWS]
        pull = own_base * moment[3:4] - 2.0 * moment
        occupied = own_base[OCCUPIED_ROW:OCCUPIED_ROW + 1] > 0
        out_ref[g] = jnp.where(occupied, 0.5 * REPEL_STRENGTH * pull, 0.0)


def forces(ghosted, local_ids):
    tiles_dev = local_ids.shape[0]
    all_tiles = ghosted.shape[1]
    group = 4
    state = ghosted[3]
    limits = jnp.where(state == 1, ADHERE_RADIUS / REPEL_RADIUS, -FAR)
    blank = jnp.zeros_like(limits)
    base = jnp.stack(
        [ghosted[0], ghosted[1], ghosted[2], state, limits, blank, blank, blank], 1
    )
    out = pl.pallas_call(
        lambda *refs: force_kernel(group, *refs),
        grid_spec=pltpu.PrefetchScalarGridSpec(
            num_scalar_prefetch=1,
            grid=(tiles_dev // group,),
            in_specs=[pl.BlockSpec((all_tiles, ROWS, TILE), lambda i, ids: (0, 0, 0))],
            out_specs=pl.BlockSpec((group, ROWS, TILE), lambda i, ids: (i, 0, 0)),
            scratch_shapes=[
                pltpu.VMEM((all_tiles, K_ROWS, TILE), jnp.bfloat16),
                pltpu.VMEM((all_tiles, Q_ROWS, TILE), jnp.bfloat16),
                pltpu.VMEM((group, TILE, 2 * NB * TILE), jnp.bfloat16),
                pltpu.VMEM((group, Q_ROWS, 2 * NB * TILE), jnp.bfloat16),
                pltpu.VMEM((group, TILE, TILE), jnp.float32),
            ],
        ),
        out_shape=jax.ShapeDtypeStruct((tiles_dev, ROWS, TILE), jnp.float32),
        cost_estimate=pl.CostEstimate(
            flops=100_000_000_000, bytes_accessed=2_000_000, transcendentals=0
        ),
        name="forces",
    )(local_ids.reshape(-1), base)
    return out[:, :3].transpose(1, 0, 2)


def count_kernel(rows, columns, column_ref, z_ref, out_ref):
    @pl.when(pl.program_id(0) == 0)
    def _():
        out_ref[...] = jnp.zeros_like(out_ref)

    def one_hot(size, ref):
        index = lax.broadcasted_iota(jnp.int32, (size, TILE), 0)
        return jnp.concatenate(
            [
                jnp.where(index == ref[r:r + 1, :], 1.0, 0.0).astype(jnp.bfloat16)
                for r in range(rows)
            ],
            1,
        )

    out_ref[...] += lax.dot_general(
        one_hot(columns, column_ref), one_hot(out_ref.shape[1], z_ref),
        (((1,), (1,)), ((), ())), preferred_element_type=jnp.float32,
    )


def count_cells(column, z, columns, size_z):
    rows = 8
    tiles_dev = column.shape[0]
    spec = pl.BlockSpec((rows, TILE), lambda i: (i, 0))
    return pl.pallas_call(
        lambda *refs: count_kernel(rows, columns, *refs),
        grid=(tiles_dev // rows,),
        in_specs=[spec, spec],
        out_specs=pl.BlockSpec((columns, size_z), lambda i: (0, 0)),
        out_shape=jax.ShapeDtypeStruct((columns, size_z), jnp.float32),
        cost_estimate=pl.CostEstimate(
            flops=20_000_000_000, bytes_accessed=1_000_000, transcendentals=0
        ),
        name="count",
    )(column, z)


def gather_kernel(slab_count, sub_count, mine_ref, all_ref, landed, send_sem, recv_sem):
    me = lax.axis_index("slab") * sub_count + lax.axis_index("sub")
    count = slab_count * sub_count

    def peer(step):
        other = lax.rem(me + step, count)
        return {"slab": other // sub_count, "sub": lax.rem(other, sub_count)}

    barrier = pltpu.get_barrier_semaphore()

    @pl.loop(1, count)
    def _(step):
        pl.semaphore_signal(
            barrier, inc=1, device_id=peer(step), device_id_type=pl.DeviceIdType.MESH
        )

    pl.semaphore_wait(barrier, count - 1)

    def copy(step):
        return pltpu.make_async_remote_copy(
            src_ref=mine_ref,
            dst_ref=landed.at[step],
            send_sem=send_sem.at[step],
            recv_sem=recv_sem.at[step],
            device_id=peer(step),
            device_id_type=pl.DeviceIdType.MESH,
        )

    @pl.loop(1, count)
    def _(step):
        copy(step).start()

    landed[0] = mine_ref[...]

    @pl.loop(1, count)
    def _(step):
        copy(step).wait()

    all_ref[...] = landed[...]


def gather_stats(stats, slab_count, sub_count):
    count = slab_count * sub_count
    vmem = pl.BlockSpec(memory_space=pltpu.VMEM)
    return pl.pallas_call(
        lambda *refs: gather_kernel(slab_count, sub_count, *refs),
        in_specs=[vmem],
        out_specs=vmem,
        out_shape=jax.ShapeDtypeStruct((count,) + stats.shape, stats.dtype),
        scratch_shapes=[
            pltpu.VMEM((count,) + stats.shape, stats.dtype),
            pltpu.SemaphoreType.DMA((count,)),
            pltpu.SemaphoreType.DMA((count,)),
        ],
        compiler_params=pltpu.CompilerParams(collective_id=0, has_side_effects=True),
        cost_estimate=pl.CostEstimate(
            flops=10_000_000_000, bytes_accessed=1_000_000, transcendentals=0
        ),
        name="gather",
    )(stats)


def neighbour_sum(padded):
    center = padded[1:-1, 1:-1]
    along_z = jnp.pad(center, ((0, 0), (0, 0), (1, 1)))
    return (
        padded[2:, 1:-1]
        + padded[:-2, 1:-1]
        + padded[1:-1, 2:]
        + padded[1:-1, :-2]
        + along_z[:, :, 2:]
        + along_z[:, :, :-2]
    )


def body(position, state, neighbours, voxel, substrate, secretion):
    tiles_dev = position.shape[1]
    sub_count = lax.axis_size("sub")
    slab_count = lax.axis_size("slab")
    slab_index = lax.axis_index("slab")
    sub_index = lax.axis_index("sub")
    live_local = jnp.sum((state == 1).astype(jnp.int32))
    necrotic_local = jnp.sum((state == 2).astype(jnp.int32))
    features = jnp.concatenate([position, state.astype(jnp.float32)[None]], 0)
    ghosted = with_halo(features, (("slab", 1),), GHOST)
    first_tile = (slab_index * sub_count + sub_index) * tiles_dev
    below_block = neighbours < first_tile
    above_block = neighbours >= first_tile + tiles_dev
    local_ids = jnp.where(
        below_block,
        neighbours - (first_tile - sub_count * tiles_dev) - (tiles_dev - GHOST),
        jnp.where(
            above_block,
            GHOST + tiles_dev + neighbours - (first_tile + sub_count * tiles_dev),
            GHOST + neighbours - first_tile,
        ),
    )
    velocity = forces(ghosted, local_ids)
    local_fastest = jnp.sqrt(jnp.max(jnp.sum(velocity * velocity, 0)))
    stats = jnp.stack(
        [live_local.astype(jnp.float32), necrotic_local.astype(jnp.float32), local_fastest]
    )
    stats = jnp.broadcast_to(jnp.pad(stats, (0, ROWS - 3))[:, None], (ROWS, TILE))
    everyone = gather_stats(stats, slab_count, sub_count)[:, :, 0]
    live_float = jnp.sum(everyone[:, 0].astype(jnp.int32)).astype(jnp.float32)
    necrotic_float = jnp.sum(everyone[:, 1].astype(jnp.int32)).astype(jnp.float32)
    fastest = jnp.max(everyone[:, 2])
    size_x, size_y, size_z = substrate.shape
    grid_y = size_y * sub_count
    grid_total = size_x * slab_count * grid_y * size_z
    per_cell = UPTAKE_SCALE * grid_total / live_float
    voxel_x = voxel // (grid_y * size_z)
    voxel_y = voxel // size_z % grid_y
    voxel_z = voxel % size_z
    column = (voxel_x - slab_index * size_x) * size_y + (voxel_y - sub_index * size_y)
    column = jnp.where(state == 1, column, -1)
    cell_count = count_cells(column, voxel_z, size_x * size_y, size_z).reshape(substrate.shape)
    right_side = substrate + SUBSTRATE_STEP * secretion
    depth = 4
    sides = (("slab", 1), ("sub", 2))
    wide = with_halo(jnp.stack([substrate, right_side, cell_count]), sides, depth)
    row_index = slab_index * size_x - depth + jnp.arange(size_x + 2 * depth)
    column_index = sub_index * size_y - depth + jnp.arange(size_y + 2 * depth)
    inside_x = (row_index >= 0) & (row_index < size_x * slab_count)
    inside_y = (column_index >= 0) & (column_index < grid_y)
    inside = inside_x[:, None, None] & inside_y[None, :, None]
    diagonal = 1.0 + SUBSTRATE_STEP * DECAY_RATE + 6.0 * DIFFUSION_NUMBER + per_cell * wide[2]
    inverse = jnp.where(inside, 1.0 / diagonal, 0.0)
    right_wide = wide[1] * inverse
    double_inverse = DIFFUSION_NUMBER * inverse
    concentration = wide[0]
    for sweep in range(SWEEPS):
        if sweep and sweep % depth == 0:
            concentration = with_halo(concentration, (("slab", 0), ("sub", 1)), depth)
        cut = sweep % depth + 1
        concentration = (
            right_wide[cut:-cut, cut:-cut]
            + double_inverse[cut:-cut, cut:-cut] * neighbour_sum(concentration)
        )
    step_size = SPEED_LIMIT / (fastest + SPEED_EPSILON)
    new_position = position + step_size * velocity
    necrotic_fraction = necrotic_float / (live_float + necrotic_float)
    return (new_position, concentration, necrotic_fraction)


def solution(mesh):
    return jax.shard_map(
        body,
        mesh=mesh,
        in_specs=(
            P(None, ("slab", "sub"), None),
            P(("slab", "sub"), None),
            P(("slab", "sub"), None),
            P(("slab", "sub"), None),
            P("slab", "sub", None),
            P("slab", "sub", None),
        ),
        out_specs=(P(None, ("slab", "sub"), None), P("slab", "sub", None), P()),
        check_vma=False,
    )
```

time: 678 us -> 256 us (0.38)
  other arithmetic: 435 us -> 21.8 us
  Pallas kernels: 0 us -> 179 us
  blocking collectives: 86.3 us -> 0 us
  local copies, waits for them, and re-layouts: 80.3 us -> 12.8 us
  starting transfers between devices: 49.8 us -> 22.1 us
    reduce_sum x17 -> x2, other arithmetic: 227 us -> 2.19 us  [the longest x1 1.54 us: body(): local_fastest = jnp.sqrt(jnp.max(jnp.sum(velocity * velocity, 0)))]
    pallas_call x0 -> x3, Pallas kernels: none -> 179 us  [the longest x1 143 us: forces(): pl.pallas_call(lambda *refs: force_kernel(group, *refs), grid_spec=pltpu....]
    scatter-add x1 -> x0, other arithmetic: 171 us -> none  [body(): cell_count = jnp.zeros((size_x * size_y * size_z,), jnp.float32).at[local...]
    psum x1 -> x0, blocking collectives: 43.9 us -> none  [body(): lax.psum((live_local, necrotic_local), ('slab', 'sub'))]
    pmax x1 -> x0, blocking collectives: 42.4 us -> none  [body(): fastest = lax.pmax(local_fastest, ('slab', 'sub'))]
    gather x16 -> x0, local copies, waits for them, and re-layouts: 31.4 us -> none  [one_block(): jnp.take(ghosted, tile_ids.reshape(-1), axis=1)]
    dynamic_slice x32 -> x0, local copies, waits for them, and re-layouts: 23.8 us -> none  [body(): forces = lax.map(one_block, (own_blocks, id_blocks))]
    ppermute x11 -> x5, starting transfers between devices: 35.4 us -> 15.5 us  [with_halo(): before = lax.ppermute(last, axis, up)]
  transfers between devices with their start and end apart: 22 -> 10, of which waited for: 7 -> 3; matrix products, arithmetic and copies ran while one was open for 74% -> 6% of each run, Pallas kernels for 0% -> 71%
where the time goes in v1:
time: 256 us; the launch traced here: 253 us
  Pallas kernels  179 us (70%)
  starting transfers between devices  22.1 us (9%)
  other arithmetic  21.8 us (9%)
  local copies, waits for them, and re-layouts  12.8 us (5%)
  waiting for transfers between devices  11.8 us (5%)
  between operations  6.17 us (2%)
    pallas_call x1, Pallas kernels, forces(): pl.pallas_call(lambda *refs: force_kernel(group, *refs), grid_spec=pltpu....  143 us
    pallas_call x1, Pallas kernels, count_cells(): pl.pallas_call(lambda *refs: count_kernel(rows, columns, *refs), grid=(ti...  20.5 us
    pallas_call x1, Pallas kernels, gather_stats(): pl.pallas_call(lambda *refs: gather_kernel(slab_count, sub_count, *refs),...  15.6 us
    ppermute x5, starting transfers between devices, with_halo(): before = lax.ppermute(last, axis, up)  15.5 us
    ppermute x5, waiting for transfers between devices, with_halo(): after = lax.ppermute(initial, axis, down)  8.05 us
    add x8, other arithmetic, body(): right_wide[cut:-cut, cut:-cut]  7.13 us
    ppermute x5, starting transfers between devices, with_halo(): after = lax.ppermute(initial, axis, down)  6.63 us
  transfers between devices with their start and end apart: 10, of which 3 were waited for; matrix products, arithmetic and copies ran while one was open for 6% of the time, Pallas kernels for 71%

profile of v1, /device:TPU:0, one launch (start us, length us, event | category | flops | bytes accessed | tf_op | source)
XLA Modules:
  0.0 253.3 jit_solution(5923591283403752110)
XLA Ops:
  0.6 2.6 %fusion.41 = (s32[256,128]{1,0:T(8,128)}, pred[256,128]{1,0:T(8,128)(4,1)S(1)}, s32[256,128]{1,0:T(8,128)}, f32[1,256,128]{2,1,0:T(8,128)S(1)}, s32[]{:T(128)}) fusion(s32[256,128]{1,0:T(8,128)} %param.9, s32[]{:T(128)S(6)} %mul.90, s32[]{:T(128)S(6)} %mul.87, s32[256,128]{1,0:T(8,128)} %param.7), kind=kLoop, calls=%fused_computation.109 | loop fusion | flops 1638399 | bytes 688140 | tf_op jit(solution)/shard_map/jit(_where)/select_n | solution.py:316
  3.3 0.8 pad_maximum_fusion.13
  4.1 4.9 %collective-permute-start = (f32[4,32,128]{2,1,0:T(8,128)S(1)}, f32[4,32,128]{2,1,0:T(8,128)S(1)}, u32[]{:S(2)}, u32[]{:S(2)}) collective-permute-start(f32[4,32,128]{2,1,0:T(8,128)S(1)} %get-tuple-element.30), channel_id=1, source_target_pairs={{0,2},{2,4},{4,6},{6,8},{8,10},{10,12},{12,14},{14,16},{16,18},{18... | collective-permute-start | bytes 196616 | tf_op jit(solution)/shard_map/ppermute | solution.py:34
  9.0 1.3 collective-permute-start.1
  10.3 0.0 copy-start
  10.3 0.0 copy-start.4
  10.3 20.5 %count.1 = f32[512,256]{1,0:T(8,128)} custom-call(s32[256,128]{1,0:T(8,128)} %get-tuple-element.14.refs_0_, s32[256,128]{1,0:T(8,128)} %get-tuple-element.32.refs_1_), custom_call_target="tpu_custom_call" | custom-call | flops 20000000000 | bytes 1000000 | tf_op jit(solution)/shard_map/count/pallas_call | solution.py:188
  30.8 0.1 add_bitcast_fusion
  30.9 1.0 copy-done.1
  31.9 0.1 pad_maximum_fusion.1
  32.0 0.0 copy-start.5
  32.0 1.3 fusion.46
  33.3 4.6 %collective-permute-start.2 = (f32[3,4,64,256]{3,2,1,0:T(8,128)}, f32[3,4,64,256]{3,2,1,0:T(8,128)S(1)}, u32[]{:S(2)}, u32[]{:S(2)}) collective-permute-start(f32[3,4,64,256]{3,2,1,0:T(8,128)} %get-tuple-element.20), channel_id=1, source_target_pairs={{0,2},{2,4},{4,6},{6,8},{8,10},{10,12},{12,14},{14,16},{16,18},{18... | collective-permute-start | bytes 2359304 | tf_op jit(solution)/shard_map/ppermute | solution.py:34
  37.9 1.3 collective-permute-start.3
  39.3 0.1 copy.21
  39.4 0.7 reshape.77.refs_0_
  40.8 0.1 broadcast_and_fusion
  40.8 0.7 convert_reduce_fusion.1
  42.2 0.8 fusion.47
  43.0 0.9 compare_select_fusion
  43.9 0.7 stack.33
  44.6 0.1 stack.34
  44.7 4.3 %stack.35.refs_1_ = f32[320,8,128]{2,1,0:T(8,128)} concatenate(f32[320,1,128]{2,1,0:T(1,128)} %bitcast.47, f32[320,1,128]{2,1,0:T(1,128)} %bitcast.46, f32[320,1,128]{2,1,0:T(1,128)S(1)} %bitcast.45, f32[320,1,128]{2,1,0:T(1,128)S(1)} %bitcast.44, f32[320,1,128]{2,1,0:T(1,128)} %compare_select_fusion, f32[320,1,128]{2,1,0:T(1,128)} %stack.33, f32[320,2,128]{2,1,0:T(2,128)S(1)} %stack.34), dimensions={1} | concatenate | bytes 2621440 | tf_op jit(solution)/shard_map/stack | solution.py:136
  49.0 142.6 %forces.1 = f32[256,8,128]{2,1,0:T(8,128)} custom-call(s32[2048]{0:T(1024)} %reshape.77.refs_0_, f32[320,8,128]{2,1,0:T(8,128)} %stack.35.refs_1_), custom_call_target="tpu_custom_call" | custom-call | flops 99999997952 | bytes 2000000 | tf_op jit(solution)/shard_map/forces/pallas_call | solution.py:139
  191.5 1.5 multiply_reduce_fusion
  193.1 0.6 reduce_max.18
  194.4 0.1 select_maximum_fusion
  194.5 1.0 pad_maximum_fusion.8
  195.5 1.3 collective-permute-start.4
  196.8 1.3 collective-permute-start.5
  198.1 0.7 broadcast_in_dim.36.refs_0_
  198.8 15.6 %gather.1 = f32[32,8,128]{2,1,0:T(8,128)} custom-call(f32[8,128]{1,0:T(8,128)} %broadcast_in_dim.36.refs_0_), custom_call_target="tpu_custom_call" | custom-call | flops 10000000000 | bytes 1000000 | tf_op jit(solution)/shard_map/gather/pallas_call | solution.py:245
  214.3 1.0 copy.25
  215.4 0.6 convert_reduce_fusion.2
  216.7 1.7 pad_maximum_fusion
  218.4 0.1 slice_bitcast_fusion
  218.5 0.1 slice.374
  218.6 0.3 fusion.4
  218.9 1.1 fusion.8
  220.0 0.1 slice.379
  220.0 0.9 fusion.16
  220.9 0.1 slice.384
  221.0 0.7 fusion.24
  221.8 0.5 fusion.32
  222.3 0.8 fusion.48
  223.1 2.8 %collective-permute-start.6 = (f32[4,64,256]{2,1,0:T(8,128)}, f32[4,64,256]{2,1,0:T(8,128)S(1)}, u32[]{:S(2)}, u32[]{:S(2)}) collective-permute-start(f32[4,64,256]{2,1,0:T(8,128)} %get-tuple-element.28), channel_id=1, source_target_pairs={{0,2},{2,4},{4,6},{6,8},{8,10},{10,12},{12,14},{14,16},{16,18},{18... | collective-permute-start | bytes 786440 | tf_op jit(solution)/shard_map/ppermute | solution.py:34
  226.0 1.3 collective-permute-start.7
  227.3 0.6 slice_reduce_fusion
  228.6 3.7 %collective-permute-done.6 = f32[4,64,256]{2,1,0:T(8,128)S(1)} collective-permute-done((f32[4,64,256]{2,1,0:T(8,128)}, f32[4,64,256]{2,1,0:T(8,128)S(1)}, u32[]{:S(2)}, u32[]{:S(2)}) %collective-permute-start.6) | collective-permute-done | bytes 262176 | tf_op jit(solution)/shard_map/ppermute | solution.py:34
  232.3 7.7 %collective-permute-done.7 = f32[4,64,256]{2,1,0:T(8,128)} collective-permute-done((f32[4,64,256]{2,1,0:T(8,128)}, f32[4,64,256]{2,1,0:T(8,128)}, u32[]{:S(2)}, u32[]{:S(2)}) %collective-permute-start.7) | collective-permute-done | bytes 262176 | tf_op jit(solution)/shard_map/ppermute | solution.py:35
  240.0 1.4 pad_maximum_fusion.11
  241.4 1.9 collective-permute-start.8
  243.3 1.5 collective-permute-start.9
  244.8 0.3 bitcast_add_fusion
  245.1 0.8 copy.27
  246.5 0.3 collective-permute-done.9
  246.8 1.1 pad_maximum_fusion.2
  247.9 0.1 slice.396
  248.0 1.1 fusion.12
  249.1 0.1 slice.401
  249.2 0.9 fusion.20
  250.0 0.1 slice.406
  250.1 0.7 fusion.28
  250.9 1.3 fusion.36
  (21 shorter events, 0.2 us)
Async XLA Ops:
  4.1 38.1 %collective-permute-start = (f32[4,32,128]{2,1,0:T(8,128)S(1)}, f32[4,32,128]{2,1,0:T(8,128)S(1)}, u32[]{:S(2)}, u32[]{:S(2)}) collective-permute-start(f32[4,32,128]{2,1,0:T(8,128)S(1)} %get-tuple-element.30), channel_id=1, source_target_pairs={{0,2},{2,4},{4,6},{6,8},{8,10},{10,12},{12,14},{14,16},{16,18},{18... | collective-permute-start | bytes 196616 | tf_op jit(solution)/shard_map/ppermute | solution.py:34
  9.0 33.2 %collective-permute-start.1 = (f32[4,32,128]{2,1,0:T(8,128)S(1)}, f32[4,32,128]{2,1,0:T(8,128)S(1)}, u32[]{:S(2)}, u32[]{:S(2)}) collective-permute-start(f32[4,32,128]{2,1,0:T(8,128)S(1)} %get-tuple-element.31), channel_id=1, source_target_pairs={{2,0},{4,2},{6,4},{8,6},{10,8},{12,10},{14,12},{16,14},{18,16},{20... | collective-permute-start | bytes 196616 | tf_op jit(solution)/shard_map/ppermute | solution.py:35
  10.3 20.5 %copy-start = (f32[8,64,256]{2,1,0:T(8,128)S(1)}, f32[8,64,256]{2,1,0:T(8,128)}, u32[]{:S(2)}) copy-start(f32[8,64,256]{2,1,0:T(8,128)} %param.10) | copy-start | bytes 1572868
  10.3 20.5 %copy-start.4 = (f32[8,64,256]{2,1,0:T(8,128)S(1)}, f32[8,64,256]{2,1,0:T(8,128)}, u32[]{:S(2)}) copy-start(f32[8,64,256]{2,1,0:T(8,128)} %param.11) | copy-start | bytes 1572868
  30.8 1.0 copy-start.1
  32.0 7.2 %copy-start.5 = (s32[256,8]{0,1:T(8,128)S(1)}, s32[256,8]{0,1:T(8,128)}, u32[]{:S(2)}) copy-start(s32[256,8]{0,1:T(8,128)} %param.8) | copy-start | bytes 24580
  32.0 10.2 %copy-start.2 = (f32[3,256,128]{2,1,0:T(8,128)S(1)}, f32[3,256,128]{2,1,0:T(8,128)}, u32[]{:S(2)}) copy-start(f32[3,256,128]{2,1,0:T(8,128)} %param.6) | copy-start | bytes 1179652
  33.3 161.2 %collective-permute-start.2 = (f32[3,4,64,256]{3,2,1,0:T(8,128)}, f32[3,4,64,256]{3,2,1,0:T(8,128)S(1)}, u32[]{:S(2)}, u32[]{:S(2)}) collective-permute-start(f32[3,4,64,256]{3,2,1,0:T(8,128)} %get-tuple-element.20), channel_id=1, source_target_pairs={{0,2},{2,4},{4,6},{6,8},{8,10},{10,12},{12,14},{14,16},{16,18},{18... | collective-permute-start | bytes 2359304 | tf_op jit(solution)/shard_map/ppermute | solution.py:34
  37.9 156.6 %collective-permute-start.3 = (f32[3,4,64,256]{3,2,1,0:T(8,128)}, f32[3,4,64,256]{3,2,1,0:T(8,128)}, u32[]{:S(2)}, u32[]{:S(2)}) collective-permute-start(f32[3,4,64,256]{3,2,1,0:T(8,128)} %get-tuple-element.21), channel_id=1, source_target_pairs={{2,0},{4,2},{6,4},{8,6},{10,8},{12,10},{14,12},{16,14},{18,16},{20... | collective-permute-start | bytes 2359304 | tf_op jit(solution)/shard_map/ppermute | solution.py:35
  195.5 21.2 %collective-permute-start.4 = (f32[3,16,4,256]{3,2,1,0:T(4,128)S(1)}, f32[3,16,4,256]{3,2,1,0:T(4,128)S(1)}, u32[]{:S(2)}, u32[]{:S(2)}) collective-permute-start(f32[3,16,4,256]{3,2,1,0:T(4,128)S(1)} %get-tuple-element.18), channel_id=1, source_target_pairs={{0,1},{2,3},{4,5},{6,7},{8,9},{10,11},{12,13},{14,15},{16,17},{18,... | collective-permute-start | bytes 589832 | tf_op jit(solution)/shard_map/ppermute | solution.py:34
  196.8 19.9 %collective-permute-start.5 = (f32[3,16,4,256]{3,2,1,0:T(4,128)S(1)}, f32[3,16,4,256]{3,2,1,0:T(4,128)S(1)}, u32[]{:S(2)}, u32[]{:S(2)}) collective-permute-start(f32[3,16,4,256]{3,2,1,0:T(4,128)S(1)} %get-tuple-element.19), channel_id=1, source_target_pairs={{1,0},{3,2},{5,4},{7,6},{9,8},{11,10},{13,12},{15,14},{17,16},{19,... | collective-permute-start | bytes 589832 | tf_op jit(solution)/shard_map/ppermute | solution.py:35
  223.1 9.2 %collective-permute-start.6 = (f32[4,64,256]{2,1,0:T(8,128)}, f32[4,64,256]{2,1,0:T(8,128)S(1)}, u32[]{:S(2)}, u32[]{:S(2)}) collective-permute-start(f32[4,64,256]{2,1,0:T(8,128)} %get-tuple-element.28), channel_id=1, source_target_pairs={{0,2},{2,4},{4,6},{6,8},{8,10},{10,12},{12,14},{14,16},{16,18},{18... | collective-permute-start | bytes 786440 | tf_op jit(solution)/shard_map/ppermute | solution.py:34
  226.0 14.0 %collective-permute-start.7 = (f32[4,64,256]{2,1,0:T(8,128)}, f32[4,64,256]{2,1,0:T(8,128)}, u32[]{:S(2)}, u32[]{:S(2)}) collective-permute-start(f32[4,64,256]{2,1,0:T(8,128)} %get-tuple-element.29), channel_id=1, source_target_pairs={{2,0},{4,2},{6,4},{8,6},{10,8},{12,10},{14,12},{16,14},{18,16},{20... | collective-permute-start | bytes 786440 | tf_op jit(solution)/shard_map/ppermute | solution.py:35
  228.5 16.3 %copy-start.3 = (f32[256,8,128]{2,1,0:T(8,128)S(1)}, f32[256,8,128]{2,1,0:T(8,128)}, u32[]{:S(2)}) copy-start(f32[256,8,128]{2,1,0:T(8,128)} %forces.1) | copy-start | bytes 3145732
  241.4 5.1 %collective-permute-start.8 = (f32[16,4,256]{2,1,0:T(4,128)}, f32[16,4,256]{2,1,0:T(4,128)}, u32[]{:S(2)}, u32[]{:S(2)}) collective-permute-start(f32[16,4,256]{2,1,0:T(4,128)} %get-tuple-element.22), channel_id=1, source_target_pairs={{0,1},{2,3},{4,5},{6,7},{8,9},{10,11},{12,13},{14,15},{16,17},{18,... | collective-permute-start | bytes 196616 | tf_op jit(solution)/shard_map/ppermute | solution.py:34
  243.3 3.5 %collective-permute-start.9 = (f32[16,4,256]{2,1,0:T(4,128)}, f32[16,4,256]{2,1,0:T(4,128)}, u32[]{:S(2)}, u32[]{:S(2)}) collective-permute-start(f32[16,4,256]{2,1,0:T(4,128)} %get-tuple-element.23), channel_id=1, source_target_pairs={{1,0},{3,2},{5,4},{7,6},{9,8},{11,10},{13,12},{15,14},{17,16},{19,... | collective-permute-start | bytes 196616 | tf_op jit(solution)/shard_map/ppermute | solution.py:35
